TPU v7x, 256 devices: a whole 4x4x8 slice. The times are simulated.
256 devices in a mesh: ctx: 16 (over x_hi, y, core), head: 16 (over z, x_lo).
Axes of the slice: x: 4 (x_hi: 2, x_lo: 2; x = x_hi * 2 + x_lo), y: 4, z: 8, core: 2. Of those that a mesh axis runs over, the one named last changes fastest.
Arguments:
- queries: bfloat16 [32, 32768, 128], P('head', 'ctx'), may hold values from -6 to 6
- key_states: bfloat16 [16, 32768, 128], P('head', 'ctx'), may hold values from -6 to 6
- value_states: bfloat16 [16, 32768, 128], P('head', 'ctx'), may hold values from -6 to 6
- attn_output: bfloat16 [32768, 4096], P(('ctx', 'head')), may hold values from -6 to 6
- out_cotangent: bfloat16 [32768, 4096], P(('ctx', 'head')), may hold values from -6 to 6
- logsumexp: float32 [32, 32768], P('head', 'ctx'), may hold values from 4.5 to 6.5
- doc_start: int32 [32768], P('ctx'), may hold values from 0 to 31744, as said below
Outputs:
- grad_queries: bfloat16 [32, 32768, 128], P('head', 'ctx')
- grad_keys: bfloat16 [16, 32768, 128], P('head', 'ctx')
- grad_values: bfloat16 [16, 32768, 128], P('head', 'ctx')
Inputs may be any that keep to these rules, and one draw needn't show every extreme that they name: doc_start[t] <= t and never falls; each value is the first position of a document; doc_start[0] = 0; the last 1024 positions form one document that starts at 31744; every other document has half of 1024 to 3072 tokens, except that the one just before the last may be shorter.
All inputs are finite; a program needn't handle non-finite values.
Results may differ from a plain program's by a relative error of at most 0.0049.
Values may be sent and summed in bfloat16 or wider, within the bound.
A program may use at most 64 MiB of HBM per device.

v0:
```python
import jax
import jax.numpy as jnp
from jax import lax
from jax.sharding import PartitionSpec as P

W = 1024
QPRE = 168


def from_behind(block, axis, distance):
    devices = range(lax.axis_size(axis))
    route = [(i - distance, i) for i in devices if i - distance in devices]
    return lax.ppermute(block, axis, route)


def band_tile(
    query_block, cotan_block, lse_block, delta_block, key_block, value_block, allowed, score_scale
):
    scores = (
        jnp.einsum("kgrd,kjd->kgrj", query_block, key_block, preferred_element_type=jnp.float32)
        * score_scale
    )
    probs = jnp.where(allowed, jnp.exp(scores - lse_block[..., None]), jnp.float32(0.0))
    probs_low = probs.astype(jnp.bfloat16)
    dprobs = jnp.einsum(
        "rkgd,kjd->kgrj", cotan_block, value_block, preferred_element_type=jnp.float32
    )
    dscores = (probs * (dprobs - delta_block[..., None])).astype(jnp.bfloat16)
    grad_value = jnp.einsum(
        "kgrj,rkgd->kjd", probs_low, cotan_block, preferred_element_type=jnp.float32
    )
    grad_key = (
        jnp.einsum("kgrj,kgrd->kjd", dscores, query_block, preferred_element_type=jnp.float32)
        * score_scale
    )
    grad_query = (
        jnp.einsum("kgrj,kjd->kgrd", dscores, key_block, preferred_element_type=jnp.float32)
        * score_scale
    )
    return (grad_query, grad_key, grad_value)


def body(queries, key_states, value_states, attn_output, out_cotangent, logsumexp, doc_start):
    kv_heads, tok_rows, head_dim = key_states.shape
    q_heads = queries.shape[0]
    groups = q_heads // kv_heads
    window = W
    block_rows = min(512, tok_rows)
    n_blocks = tok_rows // block_rows
    span = block_rows + window
    score_scale = QPRE ** (-0.5)
    shard_base = lax.axis_index("ctx") * tok_rows
    total_heads = out_cotangent.shape[1] // head_dim
    seq_cotan = out_cotangent.reshape(out_cotangent.shape[0], total_heads, head_dim)
    seq_output = attn_output.reshape(attn_output.shape[0], total_heads, head_dim)
    cotan_heads, output_heads = (
        lax.all_to_all(seq_cotan, "head", split_axis=1, concat_axis=0, tiled=True),
        lax.all_to_all(seq_output, "head", split_axis=1, concat_axis=0, tiled=True),
    )
    row_delta = jnp.sum(cotan_heads.astype(jnp.float32) * output_heads.astype(jnp.float32), axis=2)
    delta_grouped = row_delta.reshape(tok_rows, kv_heads, groups).transpose(1, 2, 0)
    lse_grouped = logsumexp.reshape(kv_heads, groups, tok_rows)
    query_grouped = queries.reshape(kv_heads, groups, tok_rows, head_dim)
    key_rim, value_rim = from_behind(
        (key_states[:, tok_rows - window :], value_states[:, tok_rows - window :]), "ctx", 1
    )
    key_ext = jnp.concatenate([key_rim, key_states], axis=1)
    value_ext = jnp.concatenate([value_rim, value_states], axis=1)
    row_iota = jnp.arange(block_rows, dtype=jnp.int32)
    col_iota = jnp.arange(span, dtype=jnp.int32)
    distance = row_iota[:, None] + window - col_iota[None, :]
    near = (distance >= 0) & (distance < window)

    def block_step(index, carry):
        grad_key_ext, grad_value_ext, grad_query_all = carry
        first = index * block_rows
        query_block = lax.dynamic_slice_in_dim(query_grouped, first, block_rows, 2)
        lse_block = lax.dynamic_slice_in_dim(lse_grouped, first, block_rows, 2)
        delta_block = lax.dynamic_slice_in_dim(delta_grouped, first, block_rows, 2)
        cotan_block = lax.dynamic_slice_in_dim(cotan_heads, first, block_rows, 0).reshape(
            block_rows, kv_heads, groups, head_dim
        )
        key_block = lax.dynamic_slice_in_dim(key_ext, first, span, 1)
        value_block = lax.dynamic_slice_in_dim(value_ext, first, span, 1)
        start_rel = lax.dynamic_slice_in_dim(doc_start, first, block_rows, 0) - shard_base
        key_local = first - window + col_iota
        allowed = near & (key_local[None, :] >= start_rel[:, None])
        grad_query, grad_key, grad_value = band_tile(
            query_block,
            cotan_block,
            lse_block,
            delta_block,
            key_block,
            value_block,
            allowed,
            score_scale,
        )
        grad_key_ext = lax.dynamic_update_slice_in_dim(
            grad_key_ext,
            lax.dynamic_slice_in_dim(grad_key_ext, first, span, 1) + grad_key,
            first,
            1,
        )
        grad_value_ext = lax.dynamic_update_slice_in_dim(
            grad_value_ext,
            lax.dynamic_slice_in_dim(grad_value_ext, first, span, 1) + grad_value,
            first,
            1,
        )
        grad_query_all = lax.dynamic_update_slice_in_dim(
            grad_query_all, grad_query.astype(jnp.bfloat16), first, 2
        )
        return (grad_key_ext, grad_value_ext, grad_query_all)

    initial = (
        jnp.zeros((kv_heads, tok_rows + window, head_dim), jnp.float32),
        jnp.zeros((kv_heads, tok_rows + window, head_dim), jnp.float32),
        jnp.zeros((kv_heads, groups, tok_rows, head_dim), jnp.bfloat16),
    )
    grad_key_ext, grad_value_ext, grad_query_all = lax.fori_loop(0, n_blocks, block_step, initial)
    back_key, back_value = from_behind(
        (grad_key_ext[:, :window], grad_value_ext[:, :window]), "ctx", -1
    )
    own_key = grad_key_ext[:, window:]
    own_value = grad_value_ext[:, window:]
    grad_keys = jnp.concatenate(
        [own_key[:, : tok_rows - window], own_key[:, tok_rows - window :] + back_key], axis=1
    )
    grad_values = jnp.concatenate(
        [own_value[:, : tok_rows - window], own_value[:, tok_rows - window :] + back_value], axis=1
    )
    grad_queries = grad_query_all.reshape(q_heads, tok_rows, head_dim)
    return (grad_queries, grad_keys.astype(jnp.bfloat16), grad_values.astype(jnp.bfloat16))


def solution(mesh):
    return jax.shard_map(
        body,
        mesh=mesh,
        in_specs=(
            P("head", "ctx", None),
            P("head", "ctx", None),
            P("head", "ctx", None),
            P(("ctx", "head"), None),
            P(("ctx", "head"), None),
            P("head", "ctx"),
            P("ctx"),
        ),
        out_specs=(P("head", "ctx", None), P("head", "ctx", None), P("head", "ctx", None)),
        check_vma=False,
    )
```

profile of v0, /device:TPU:25, one launch (start us, length us, event | category | flops | bytes accessed | tf_op | source)
XLA Modules:
  0.0 144.7 jit_solution(6352364659032542648)
XLA Ops:
  0.6 2.3 %copy.27 = bf16[128,4096]{0,1:T(8,128)(2,1)} copy(bf16[128,4096]{1,0:T(8,128)(2,1)} %param.13) | data formatting | bytes 2097152 | tf_op args[4]
  2.9 9.3 %all-to-all-start = ((bf16[128,32,128]{0,2,1:T(8,128)(2,1)}), bf16[128,32,128]{0,2,1:T(8,128)(2,1)S(1)}, u32[]{:S(2)}, u32[]{:S(2)}) async-start(bf16[128,32,128]{0,2,1:T(8,128)(2,1)} %bitcast.2), calls=%async_computation | async-start | bytes 2097152 | tf_op jit(solution)/shard_map/all_to_all | solution.py:57
  12.3 2.3 %copy.30 = bf16[128,4096]{0,1:T(8,128)(2,1)} copy(bf16[128,4096]{1,0:T(8,128)(2,1)} %param.12) | data formatting | bytes 2097152 | tf_op args[3]
  14.5 23.0 %all-to-all-done = bf16[128,32,128]{0,2,1:T(8,128)(2,1)S(1)} async-done(((bf16[128,32,128]{0,2,1:T(8,128)(2,1)}), bf16[128,32,128]{0,2,1:T(8,128)(2,1)S(1)}, u32[]{:S(2)}, u32[]{:S(2)}) %all-to-all-start) | async-done | bytes 1048608 | tf_op jit(solution)/shard_map/all_to_all | solution.py:57
  37.6 6.4 %all-to-all-start.1 = ((bf16[128,32,128]{0,2,1:T(8,128)(2,1)}), bf16[128,32,128]{0,2,1:T(8,128)(2,1)}, u32[]{:S(2)}, u32[]{:S(2)}) async-start(bf16[128,32,128]{0,2,1:T(8,128)(2,1)} %bitcast.8), calls=%async_computation.1 | async-start | bytes 2097152 | tf_op jit(solution)/shard_map/all_to_all | solution.py:58
  44.0 6.2 %collective-permute-start = (bf16[1,1024,128]{2,1,0:T(8,128)(2,1)S(1)}, bf16[1,1024,128]{2,1,0:T(8,128)(2,1)}, u32[]{:S(2)}, u32[]{:S(2)}) collective-permute-start(bf16[1,1024,128]{2,1,0:T(8,128)(2,1)S(1)} %slice.32), channel_id=1, source_target_pairs={{0,16},{16,32},{32,48},{48,64},{64,80},{80,96},{96,112},{112,128},... | collective-permute-start | bytes 786440 | tf_op jit(solution)/shard_map/ppermute | solution.py:13
  50.2 1.9 %collective-permute-start.1 = (bf16[1,1024,128]{2,1,0:T(8,128)(2,1)S(1)}, bf16[1,1024,128]{2,1,0:T(8,128)(2,1)S(1)}, u32[]{:S(2)}, u32[]{:S(2)}) collective-permute-start(bf16[1,1024,128]{2,1,0:T(8,128)(2,1)S(1)} %slice.33), channel_id=1, source_target_pairs={{0,16},{16,32},{32,48},{48,64},{64,80},{80,96},{96,112},{112,128},... | collective-permute-start | bytes 786440 | tf_op jit(solution)/shard_map/ppermute | solution.py:13
  52.2 1.8 %collective-permute-done = bf16[1,1024,128]{2,1,0:T(8,128)(2,1)} collective-permute-done((bf16[1,1024,128]{2,1,0:T(8,128)(2,1)S(1)}, bf16[1,1024,128]{2,1,0:T(8,128)(2,1)}, u32[]{:S(2)}, u32[]{:S(2)}) %collective-permute-start) | collective-permute-done | bytes 262176 | tf_op jit(solution)/shard_map/ppermute | solution.py:13
  55.0 2.1 %collective-permute-done.1 = bf16[1,1024,128]{2,1,0:T(8,128)(2,1)S(1)} collective-permute-done((bf16[1,1024,128]{2,1,0:T(8,128)(2,1)S(1)}, bf16[1,1024,128]{2,1,0:T(8,128)(2,1)S(1)}, u32[]{:S(2)}, u32[]{:S(2)}) %collective-permute-start.1) | collective-permute-done | bytes 262176 | tf_op jit(solution)/shard_map/ppermute | solution.py:13
  58.1 1.3 copy.29
  59.4 1.3 copy.28
  60.7 7.7 %all-to-all-done.1 = bf16[128,32,128]{0,2,1:T(8,128)(2,1)} async-done(((bf16[128,32,128]{0,2,1:T(8,128)(2,1)}), bf16[128,32,128]{0,2,1:T(8,128)(2,1)}, u32[]{:S(2)}, u32[]{:S(2)}) %all-to-all-start.1) | async-done | bytes 1048608 | tf_op jit(solution)/shard_map/all_to_all | solution.py:58
  68.4 1.5 %copy.31 = f32[128,32,128]{2,0,1:T(8,128)S(1)} copy(bf16[128,32,128]{0,2,1:T(8,128)(2,1)} %all-to-all-done.1) | data formatting | bytes 3145728 | tf_op jit(solution)/shard_map/convert_element_type | solution.py:60
  69.9 1.8 %multiply_reduce_fusion = f32[16,128,2]{1,2,0:T(2,128)S(1)} fusion(f32[16,128,2,128]{3,1,2,0:T(8,128)S(1)} %bitcast.111, bf16[16,128,2,128]{3,1,2,0:T(8,128)(2,1)} %bitcast.113), kind=kLoop, calls=%fused_computation.51 | loop fusion | flops 1568768 | bytes 3162112 | tf_op jit(solution)/shard_map/reduce_sum | solution.py:60
  74.2 47.9 %while.20 = (s32[]{:T(128)}, f32[1,3072,128]{2,1,0:T(8,128)S(1)}, f32[1,3072,128]{2,1,0:T(8,128)}, bf16[1,2,2048,128]{3,2,1,0:T(8,128)(2,1)}, s32[2048]{0:T(1024...) while((s32[]{:T(128)}, f32[1,3072,128]{2,1,0:T(8,128)S(1)}, ...), condition=%wide.region_2.3_spmd.clone, body=%wide.region_1.2_spmd.clone.sunk | while | flops 2034567168 | bytes 56279464 | solution.py:120
  75.7 1.3 fusion.80
  78.7 2.2 %fusion.83 = f32[1,3072,128]{2,1,0:T(8,128)S(1)} fusion(f32[1,3072,128]{2,1,0:T(8,128)S(1)} %copy-done.1, s32[]{:T(128)S(6)} %select_n.68, f32[2,512,1536]{2,1,0:T(8,128)S(1)} %fusion.79, f32[2,512]{1,0:T(2,128)S(1)} %get-tuple-element.478, pred[512,1536]{1,0:T(8,128)(4,1)S(1)} %fusion.80, bf16[2048,2,128]{2,0,1:T(8,128)(2,1)S(1)} %copy-done.5, ...), kind=kOutput, calls=%fused_computation.17.clone.1 | convolution fusion | flops 409141248 | bytes 8917000 | tf_op jit(solution)/shard_map/while/body/eval_jaxpr/kgrj,rkgd->kjd/dot_general | solution.py:29
  80.9 2.5 %fusion.81 = bf16[2,512,1536]{2,1,0:T(8,128)(2,1)S(1)} fusion(f32[2,512,1536]{2,1,0:T(8,128)S(1)} %fusion.79, f32[2,512]{1,0:T(2,128)S(1)} %get-tuple-element.477, f32[2,512]{1,0:T(2,128)S(1)} %get-tuple-element.478, pred[512,1536]{1,0:T(8,128)(4,1)S(1)} %fusion.80, bf16[1,3072,128]{2,1,0:T(8,128)(2,1)S(1)} %copy-done.6, s32[]{:T(128)S(6)} %select_n.68, ...), kind=kOutput, calls=%fused_computation.7.clone.1 | convolution fusion | flops 412090368 | bytes 10887176 | tf_op jit(solution)/shard_map/while/body/eval_jaxpr/rkgd,kjd->kgrj/dot_general | solution.py:25
  83.5 1.7 %fusion.84 = bf16[1,2,2048,128]{3,2,1,0:T(8,128)(2,1)} fusion(bf16[1,2,2048,128]{3,2,1,0:T(8,128)(2,1)} %get-tuple-element.501, s32[]{:T(128)S(6)} %select_n.69, bf16[2,512,1536]{2,1,0:T(8,128)(2,1)S(1)} %fusion.81, bf16[1,3072,128]{2,1,0:T(8,128)(2,1)S(1)} %get-tuple-element.524, s32[]{:T(128)S(6)} %select_n.68), kind=kOutput, calls=%fused_computation.26.clone.1 | convolution fusion | flops 402915328 | bytes 3801096 | tf_op jit(solution)/shard_map/while/body/eval_jaxpr/kgrj,kjd->kgrd/dot_general | solution.py:37
  90.7 2.2 %fusion.83 = f32[1,3072,128]{2,1,0:T(8,128)S(1)} fusion(f32[1,3072,128]{2,1,0:T(8,128)S(1)} %copy-done.1, s32[]{:T(128)S(6)} %select_n.68, f32[2,512,1536]{2,1,0:T(8,128)S(1)} %fusion.79, f32[2,512]{1,0:T(2,128)S(1)} %get-tuple-element.478, pred[512,1536]{1,0:T(8,128)(4,1)S(1)} %fusion.80, bf16[2048,2,128]{2,0,1:T(8,128)(2,1)S(1)} %copy-done.5, ...), kind=kOutput, calls=%fused_computation.17.clone.1 | convolution fusion | flops 409141248 | bytes 8917000 | tf_op jit(solution)/shard_map/while/body/eval_jaxpr/kgrj,rkgd->kjd/dot_general | solution.py:29
  92.9 2.5 %fusion.81 = bf16[2,512,1536]{2,1,0:T(8,128)(2,1)S(1)} fusion(f32[2,512,1536]{2,1,0:T(8,128)S(1)} %fusion.79, f32[2,512]{1,0:T(2,128)S(1)} %get-tuple-element.477, f32[2,512]{1,0:T(2,128)S(1)} %get-tuple-element.478, pred[512,1536]{1,0:T(8,128)(4,1)S(1)} %fusion.80, bf16[1,3072,128]{2,1,0:T(8,128)(2,1)S(1)} %copy-done.6, s32[]{:T(128)S(6)} %select_n.68, ...), kind=kOutput, calls=%fused_computation.7.clone.1 | convolution fusion | flops 412090368 | bytes 10887176 | tf_op jit(solution)/shard_map/while/body/eval_jaxpr/rkgd,kjd->kgrj/dot_general | solution.py:25
  95.4 1.7 %fusion.84 = bf16[1,2,2048,128]{3,2,1,0:T(8,128)(2,1)} fusion(bf16[1,2,2048,128]{3,2,1,0:T(8,128)(2,1)} %get-tuple-element.501, s32[]{:T(128)S(6)} %select_n.69, bf16[2,512,1536]{2,1,0:T(8,128)(2,1)S(1)} %fusion.81, bf16[1,3072,128]{2,1,0:T(8,128)(2,1)S(1)} %get-tuple-element.524, s32[]{:T(128)S(6)} %select_n.68), kind=kOutput, calls=%fused_computation.26.clone.1 | convolution fusion | flops 402915328 | bytes 3801096 | tf_op jit(solution)/shard_map/while/body/eval_jaxpr/kgrj,kjd->kgrd/dot_general | solution.py:37
  102.6 2.2 %fusion.83 = f32[1,3072,128]{2,1,0:T(8,128)S(1)} fusion(f32[1,3072,128]{2,1,0:T(8,128)S(1)} %copy-done.1, s32[]{:T(128)S(6)} %select_n.68, f32[2,512,1536]{2,1,0:T(8,128)S(1)} %fusion.79, f32[2,512]{1,0:T(2,128)S(1)} %get-tuple-element.478, pred[512,1536]{1,0:T(8,128)(4,1)S(1)} %fusion.80, bf16[2048,2,128]{2,0,1:T(8,128)(2,1)S(1)} %copy-done.5, ...), kind=kOutput, calls=%fused_computation.17.clone.1 | convolution fusion | flops 409141248 | bytes 8917000 | tf_op jit(solution)/shard_map/while/body/eval_jaxpr/kgrj,rkgd->kjd/dot_general | solution.py:29
  104.9 2.5 %fusion.81 = bf16[2,512,1536]{2,1,0:T(8,128)(2,1)S(1)} fusion(f32[2,512,1536]{2,1,0:T(8,128)S(1)} %fusion.79, f32[2,512]{1,0:T(2,128)S(1)} %get-tuple-element.477, f32[2,512]{1,0:T(2,128)S(1)} %get-tuple-element.478, pred[512,1536]{1,0:T(8,128)(4,1)S(1)} %fusion.80, bf16[1,3072,128]{2,1,0:T(8,128)(2,1)S(1)} %copy-done.6, s32[]{:T(128)S(6)} %select_n.68, ...), kind=kOutput, calls=%fused_computation.7.clone.1 | convolution fusion | flops 412090368 | bytes 10887176 | tf_op jit(solution)/shard_map/while/body/eval_jaxpr/rkgd,kjd->kgrj/dot_general | solution.py:25
  107.4 1.7 %fusion.84 = bf16[1,2,2048,128]{3,2,1,0:T(8,128)(2,1)} fusion(bf16[1,2,2048,128]{3,2,1,0:T(8,128)(2,1)} %get-tuple-element.501, s32[]{:T(128)S(6)} %select_n.69, bf16[2,512,1536]{2,1,0:T(8,128)(2,1)S(1)} %fusion.81, bf16[1,3072,128]{2,1,0:T(8,128)(2,1)S(1)} %get-tuple-element.524, s32[]{:T(128)S(6)} %select_n.68), kind=kOutput, calls=%fused_computation.26.clone.1 | convolution fusion | flops 402915328 | bytes 3801096 | tf_op jit(solution)/shard_map/while/body/eval_jaxpr/kgrj,kjd->kgrd/dot_general | solution.py:37
  114.6 2.2 %fusion.83 = f32[1,3072,128]{2,1,0:T(8,128)S(1)} fusion(f32[1,3072,128]{2,1,0:T(8,128)S(1)} %copy-done.1, s32[]{:T(128)S(6)} %select_n.68, f32[2,512,1536]{2,1,0:T(8,128)S(1)} %fusion.79, f32[2,512]{1,0:T(2,128)S(1)} %get-tuple-element.478, pred[512,1536]{1,0:T(8,128)(4,1)S(1)} %fusion.80, bf16[2048,2,128]{2,0,1:T(8,128)(2,1)S(1)} %copy-done.5, ...), kind=kOutput, calls=%fused_computation.17.clone.1 | convolution fusion | flops 409141248 | bytes 8917000 | tf_op jit(solution)/shard_map/while/body/eval_jaxpr/kgrj,rkgd->kjd/dot_general | solution.py:29
  116.8 2.5 %fusion.81 = bf16[2,512,1536]{2,1,0:T(8,128)(2,1)S(1)} fusion(f32[2,512,1536]{2,1,0:T(8,128)S(1)} %fusion.79, f32[2,512]{1,0:T(2,128)S(1)} %get-tuple-element.477, f32[2,512]{1,0:T(2,128)S(1)} %get-tuple-element.478, pred[512,1536]{1,0:T(8,128)(4,1)S(1)} %fusion.80, bf16[1,3072,128]{2,1,0:T(8,128)(2,1)S(1)} %copy-done.6, s32[]{:T(128)S(6)} %select_n.68, ...), kind=kOutput, calls=%fused_computation.7.clone.1 | convolution fusion | flops 412090368 | bytes 10887176 | tf_op jit(solution)/shard_map/while/body/eval_jaxpr/rkgd,kjd->kgrj/dot_general | solution.py:25
  119.4 1.7 %fusion.84 = bf16[1,2,2048,128]{3,2,1,0:T(8,128)(2,1)} fusion(bf16[1,2,2048,128]{3,2,1,0:T(8,128)(2,1)} %get-tuple-element.501, s32[]{:T(128)S(6)} %select_n.69, bf16[2,512,1536]{2,1,0:T(8,128)(2,1)S(1)} %fusion.81, bf16[1,3072,128]{2,1,0:T(8,128)(2,1)S(1)} %get-tuple-element.524, s32[]{:T(128)S(6)} %select_n.68), kind=kOutput, calls=%fused_computation.26.clone.1 | convolution fusion | flops 402915328 | bytes 3801096 | tf_op jit(solution)/shard_map/while/body/eval_jaxpr/kgrj,kjd->kgrd/dot_general | solution.py:37
  123.2 6.1 %collective-permute-start.3 = (f32[1,1024,128]{2,1,0:T(8,128)S(1)}, f32[1,1024,128]{2,1,0:T(8,128)S(1)}, u32[]{:S(2)}, u32[]{:S(2)}) collective-permute-start(f32[1,1024,128]{2,1,0:T(8,128)S(1)} %slice.39), channel_id=1, source_target_pairs={{16,0},{32,16},{48,32},{64,48},{80,64},{96,80},{112,96},{128,112},... | collective-permute-start | bytes 1572872 | tf_op jit(solution)/shard_map/ppermute | solution.py:13
  129.4 1.9 %collective-permute-start.2 = (f32[1,1024,128]{2,1,0:T(8,128)S(1)}, f32[1,1024,128]{2,1,0:T(8,128)S(1)}, u32[]{:S(2)}, u32[]{:S(2)}) collective-permute-start(f32[1,1024,128]{2,1,0:T(8,128)S(1)} %slice.36), channel_id=1, source_target_pairs={{16,0},{32,16},{48,32},{64,48},{80,64},{96,80},{112,96},{128,112},... | collective-permute-start | bytes 1572872 | tf_op jit(solution)/shard_map/ppermute | solution.py:13
  132.4 5.8 %collective-permute-done.3 = f32[1,1024,128]{2,1,0:T(8,128)S(1)} collective-permute-done((f32[1,1024,128]{2,1,0:T(8,128)S(1)}, f32[1,1024,128]{2,1,0:T(8,128)S(1)}, u32[]{:S(2)}, u32[]{:S(2)}) %collective-permute-start.3) | collective-permute-done | bytes 524320 | tf_op jit(solution)/shard_map/ppermute | solution.py:13
  140.1 3.7 %collective-permute-done.2 = f32[1,1024,128]{2,1,0:T(8,128)S(1)} collective-permute-done((f32[1,1024,128]{2,1,0:T(8,128)S(1)}, f32[1,1024,128]{2,1,0:T(8,128)S(1)}, u32[]{:S(2)}, u32[]{:S(2)}) %collective-permute-start.2) | collective-permute-done | bytes 524320 | tf_op jit(solution)/shard_map/ppermute | solution.py:13
  (77 shorter events, 30.1 us)
Async XLA Ops:
  2.9 41.1 %copy-start.3 = (bf16[1,2048,128]{2,1,0:T(8,128)(2,1)S(1)}, bf16[1,2048,128]{2,1,0:T(8,128)(2,1)}, u32[]{:S(2)}) copy-start(bf16[1,2048,128]{2,1,0:T(8,128)(2,1)} %param.10) | copy-start | bytes 1572868
  2.9 47.3 %copy-start.4 = (bf16[1,2048,128]{2,1,0:T(8,128)(2,1)S(1)}, bf16[1,2048,128]{2,1,0:T(8,128)(2,1)}, u32[]{:S(2)}) copy-start(bf16[1,2048,128]{2,1,0:T(8,128)(2,1)} %param.11) | copy-start | bytes 1572868
  2.9 34.7 %all-to-all-start = ((bf16[128,32,128]{0,2,1:T(8,128)(2,1)}), bf16[128,32,128]{0,2,1:T(8,128)(2,1)S(1)}, u32[]{:S(2)}, u32[]{:S(2)}) async-start(bf16[128,32,128]{0,2,1:T(8,128)(2,1)} %bitcast.2), calls=%async_computation | async-start | bytes 2097152 | tf_op jit(solution)/shard_map/all_to_all | solution.py:57
  37.6 30.9 %all-to-all-start.1 = ((bf16[128,32,128]{0,2,1:T(8,128)(2,1)}), bf16[128,32,128]{0,2,1:T(8,128)(2,1)}, u32[]{:S(2)}, u32[]{:S(2)}) async-start(bf16[128,32,128]{0,2,1:T(8,128)(2,1)} %bitcast.8), calls=%async_computation.1 | async-start | bytes 2097152 | tf_op jit(solution)/shard_map/all_to_all | solution.py:58
  44.0 10.0 %collective-permute-start = (bf16[1,1024,128]{2,1,0:T(8,128)(2,1)S(1)}, bf16[1,1024,128]{2,1,0:T(8,128)(2,1)}, u32[]{:S(2)}, u32[]{:S(2)}) collective-permute-start(bf16[1,1024,128]{2,1,0:T(8,128)(2,1)S(1)} %slice.32), channel_id=1, source_target_pairs={{0,16},{16,32},{32,48},{48,64},{64,80},{80,96},{96,112},{112,128},... | collective-permute-start | bytes 786440 | tf_op jit(solution)/shard_map/ppermute | solution.py:13
  50.2 6.8 %collective-permute-start.1 = (bf16[1,1024,128]{2,1,0:T(8,128)(2,1)S(1)}, bf16[1,1024,128]{2,1,0:T(8,128)(2,1)S(1)}, u32[]{:S(2)}, u32[]{:S(2)}) collective-permute-start(bf16[1,1024,128]{2,1,0:T(8,128)(2,1)S(1)} %slice.33), channel_id=1, source_target_pairs={{0,16},{16,32},{32,48},{48,64},{64,80},{80,96},{96,112},{112,128},... | collective-permute-start | bytes 786440 | tf_op jit(solution)/shard_map/ppermute | solution.py:13
  71.8 2.5 %copy-start = (bf16[2,2048,128]{2,1,0:T(8,128)(2,1)S(1)}, bf16[2,2048,128]{2,1,0:T(8,128)(2,1)}, u32[]{:S(2)}) copy-start(bf16[2,2048,128]{2,1,0:T(8,128)(2,1)} %param.9) | copy-start | bytes 3145732
  77.0 1.4 copy-start.1
  77.0 1.7 %copy-start.5 = (bf16[2048,2,128]{2,0,1:T(8,128)(2,1)S(1)}, bf16[2048,2,128]{2,0,1:T(8,128)(2,1)}, u32[]{:S(2)}) copy-start(bf16[2048,2,128]{2,0,1:T(8,128)(2,1)} %get-tuple-element.527) | copy-start | bytes 3145732 | tf_op jit(solution)/shard_map/while
  78.7 2.2 %copy-start.6 = (bf16[1,3072,128]{2,1,0:T(8,128)(2,1)S(1)}, bf16[1,3072,128]{2,1,0:T(8,128)(2,1)}, u32[]{:S(2)}) copy-start(bf16[1,3072,128]{2,1,0:T(8,128)(2,1)} %get-tuple-element.526) | copy-start | bytes 2359300 | tf_op jit(solution)/shard_map/while
  80.9 2.5 %copy-start.2 = (f32[1,3072,128]{2,1,0:T(8,128)}, f32[1,3072,128]{2,1,0:T(8,128)S(1)}, u32[]{:S(2)}) copy-start(f32[1,3072,128]{2,1,0:T(8,128)S(1)} %fusion.83) | copy-start | bytes 4718596 | tf_op jit(solution)/shard_map/while
  89.0 1.4 copy-start.1
  89.0 1.7 %copy-start.5 = (bf16[2048,2,128]{2,0,1:T(8,128)(2,1)S(1)}, bf16[2048,2,128]{2,0,1:T(8,128)(2,1)}, u32[]{:S(2)}) copy-start(bf16[2048,2,128]{2,0,1:T(8,128)(2,1)} %get-tuple-element.527) | copy-start | bytes 3145732 | tf_op jit(solution)/shard_map/while
  90.7 2.2 %copy-start.6 = (bf16[1,3072,128]{2,1,0:T(8,128)(2,1)S(1)}, bf16[1,3072,128]{2,1,0:T(8,128)(2,1)}, u32[]{:S(2)}) copy-start(bf16[1,3072,128]{2,1,0:T(8,128)(2,1)} %get-tuple-element.526) | copy-start | bytes 2359300 | tf_op jit(solution)/shard_map/while
  92.9 2.5 %copy-start.2 = (f32[1,3072,128]{2,1,0:T(8,128)}, f32[1,3072,128]{2,1,0:T(8,128)S(1)}, u32[]{:S(2)}) copy-start(f32[1,3072,128]{2,1,0:T(8,128)S(1)} %fusion.83) | copy-start | bytes 4718596 | tf_op jit(solution)/shard_map/while
  100.9 1.4 copy-start.1
  100.9 1.7 %copy-start.5 = (bf16[2048,2,128]{2,0,1:T(8,128)(2,1)S(1)}, bf16[2048,2,128]{2,0,1:T(8,128)(2,1)}, u32[]{:S(2)}) copy-start(bf16[2048,2,128]{2,0,1:T(8,128)(2,1)} %get-tuple-element.527) | copy-start | bytes 3145732 | tf_op jit(solution)/shard_map/while
  102.6 2.2 %copy-start.6 = (bf16[1,3072,128]{2,1,0:T(8,128)(2,1)S(1)}, bf16[1,3072,128]{2,1,0:T(8,128)(2,1)}, u32[]{:S(2)}) copy-start(bf16[1,3072,128]{2,1,0:T(8,128)(2,1)} %get-tuple-element.526) | copy-start | bytes 2359300 | tf_op jit(solution)/shard_map/while
  104.8 2.5 %copy-start.2 = (f32[1,3072,128]{2,1,0:T(8,128)}, f32[1,3072,128]{2,1,0:T(8,128)S(1)}, u32[]{:S(2)}) copy-start(f32[1,3072,128]{2,1,0:T(8,128)S(1)} %fusion.83) | copy-start | bytes 4718596 | tf_op jit(solution)/shard_map/while
  112.9 1.4 copy-start.1
  112.9 1.7 %copy-start.5 = (bf16[2048,2,128]{2,0,1:T(8,128)(2,1)S(1)}, bf16[2048,2,128]{2,0,1:T(8,128)(2,1)}, u32[]{:S(2)}) copy-start(bf16[2048,2,128]{2,0,1:T(8,128)(2,1)} %get-tuple-element.527) | copy-start | bytes 3145732 | tf_op jit(solution)/shard_map/while
  114.6 2.2 %copy-start.6 = (bf16[1,3072,128]{2,1,0:T(8,128)(2,1)S(1)}, bf16[1,3072,128]{2,1,0:T(8,128)(2,1)}, u32[]{:S(2)}) copy-start(bf16[1,3072,128]{2,1,0:T(8,128)(2,1)} %get-tuple-element.526) | copy-start | bytes 2359300 | tf_op jit(solution)/shard_map/while
  116.8 2.5 %copy-start.2 = (f32[1,3072,128]{2,1,0:T(8,128)}, f32[1,3072,128]{2,1,0:T(8,128)S(1)}, u32[]{:S(2)}) copy-start(f32[1,3072,128]{2,1,0:T(8,128)S(1)} %fusion.83) | copy-start | bytes 4718596 | tf_op jit(solution)/shard_map/while
  123.2 15.0 %collective-permute-start.3 = (f32[1,1024,128]{2,1,0:T(8,128)S(1)}, f32[1,1024,128]{2,1,0:T(8,128)S(1)}, u32[]{:S(2)}, u32[]{:S(2)}) collective-permute-start(f32[1,1024,128]{2,1,0:T(8,128)S(1)} %slice.39), channel_id=1, source_target_pairs={{16,0},{32,16},{48,32},{64,48},{80,64},{96,80},{112,96},{128,112},... | collective-permute-start | bytes 1572872 | tf_op jit(solution)/shard_map/ppermute | solution.py:13
  129.4 14.4 %collective-permute-start.2 = (f32[1,1024,128]{2,1,0:T(8,128)S(1)}, f32[1,1024,128]{2,1,0:T(8,128)S(1)}, u32[]{:S(2)}, u32[]{:S(2)}) collective-permute-start(f32[1,1024,128]{2,1,0:T(8,128)S(1)} %slice.36), channel_id=1, source_target_pairs={{16,0},{32,16},{48,32},{64,48},{80,64},{96,80},{112,96},{128,112},... | collective-permute-start | bytes 1572872 | tf_op jit(solution)/shard_map/ppermute | solution.py:13
where the time goes:
time: 146 us; the launch traced here: 145 us
  waiting for transfers between devices  44.1 us (30%)
  matrix products  33.7 us (23%)
  starting transfers between devices  31.9 us (22%)
  local copies, waits for them, and re-layouts  18.9 us (13%)
  other arithmetic  14.9 us (10%)
    all_to_all x1, waiting for transfers between devices, body(): lax.all_to_all(seq_cotan, 'head', split_axis=1, concat_axis=0, tiled=True)  23 us
    ppermute x4, starting transfers between devices, from_behind(): return lax.ppermute(block, axis, route)  16.1 us
    ppermute x4, waiting for transfers between devices, from_behind(): return lax.ppermute(block, axis, route)  13.3 us
    dot_general x4, matrix products, band_tile(): jnp.einsum('rkgd,kjd->kgrj', cotan_block, value_block, preferred_element_...  10.1 us
    all_to_all x1, starting transfers between devices, body(): lax.all_to_all(seq_cotan, 'head', split_axis=1, concat_axis=0, tiled=True)  9.35 us
    dot_general x4, matrix products, band_tile(): jnp.einsum('kgrj,rkgd->kjd', probs_low, cotan_block, preferred_element_ty...  8.77 us
    all_to_all x1, waiting for transfers between devices, body(): lax.all_to_all(seq_output, 'head', split_axis=1, concat_axis=0, tiled=True)  7.74 us
    dot_general x4, matrix products, band_tile(): jnp.einsum('kgrj,kjd->kgrd', dscores, key_block, preferred_element_type=j...  6.76 us
  transfers between devices with their start and end apart: 6, of which 6 were waited for; matrix products, arithmetic and copies ran while one was open for 7% of the time, Pallas kernels for 0%

commit v1 on v0

v1 whole, which is shorter than its diff:
```python
import functools

import jax
import jax.numpy as jnp
from jax import lax
from jax.experimental import pallas as pl
from jax.experimental.pallas import tpu as pltpu
from jax.sharding import PartitionSpec as P

W = 1024
QPRE = 168
SCALE = QPRE ** (-0.5)
LOG2E = 1.4426950408889634
MESH = pl.DeviceIdType.MESH
BF = jnp.bfloat16
F32 = jnp.float32
NT = (((1,), (1,)), ((), ()))
NN = (((1,), (0,)), ((), ()))
PEERS = ((0, 1), (1, 0), (7, 0), (1, 1), (7, 1), (2, 0), (6, 0), (2, 1), (6, 1), (3, 0), (5, 0), (3, 1), (5, 1), (4, 0), (4, 1))


def mm(a, b, dims):
    return lax.dot_general(a, b, dims, preferred_element_type=F32)


def side(parts, axis):
    return parts[0] if len(parts) == 1 else jnp.concatenate(parts, axis=axis)


def segments(rows):
    if rows > 1152:
        return ((0, 128, "A"), (128, 1024, "AB"), (1152, 128, "B"))
    return ((0, 128, "A"), (128, rows - 128, "AB"))


def attention_kernel(
    q_hbm, k_hbm, v_hbm, out_hbm, cot_hbm, lse_hbm, doc_hbm,
    dq_hbm, dk_hbm, dv_hbm,
    qv, kx, vx, kt, outv, cotv, lsev, docv, cots, dels, delsrc, probs, dka, dva, dqo, dko, dvo,
    load_sem, halo_send, halo_recv, cot_send, cot_recv, del_send, del_recv,
    fwd_send, fwd_recv, fwd_del_send, fwd_del_recv, store_sem,
):
    ctx = lax.axis_index("ctx")
    head = lax.axis_index("head")
    z, x = head // 2, head % 2
    nxt, prv = lax.rem(ctx + 1, 16), lax.rem(ctx + 15, 16)
    peers = [lax.rem(z + dz, 8) * 2 + lax.rem(x + dx, 2) for dz, dx in PEERS]

    barrier = pltpu.get_barrier_semaphore()
    for peer in peers:
        pl.semaphore_signal(barrier, inc=1, device_id={"head": peer}, device_id_type=MESH)
    for peer in (nxt, prv):
        pl.semaphore_signal(barrier, inc=1, device_id={"ctx": peer}, device_id_type=MESH)

    loads = [
        pltpu.make_async_copy(cot_hbm, cotv, load_sem.at[0]),
        pltpu.make_async_copy(out_hbm, outv, load_sem.at[1]),
        pltpu.make_async_copy(q_hbm, qv.at[:, pl.ds(0, 2048), :], load_sem.at[2]),
        pltpu.make_async_copy(k_hbm.at[0], kx.at[pl.ds(1024, 2048), :], load_sem.at[3]),
        pltpu.make_async_copy(v_hbm.at[0], vx.at[pl.ds(1024, 2048), :], load_sem.at[4]),
        pltpu.make_async_copy(lse_hbm, lsev.at[:, pl.ds(0, 2048)], load_sem.at[5]),
        pltpu.make_async_copy(doc_hbm, docv.at[pl.ds(0, 16), :], load_sem.at[6]),
    ]
    for load in loads:
        load.start()

    loads[0].wait()
    loads[1].wait()
    lane = lax.broadcasted_iota(jnp.int32, (128, 128), 1)
    rows_delta = jnp.zeros((128, 128), F32)
    for h in range(32):
        cols = slice(h * 128, (h + 1) * 128)
        product = cotv[:, cols].astype(F32) * outv[:, cols].astype(F32)
        rows_delta = jnp.where(lane == h, jnp.sum(product, axis=1, keepdims=True), rows_delta)
    rows_delta = rows_delta.T
    for j in range(16):
        delsrc[j] = rows_delta[2 * j : 2 * j + 2]

    pl.semaphore_wait(barrier, 17)
    sends = []

    def send(src, dst, send_sem, recv_sem, where):
        copy = pltpu.make_async_remote_copy(
            src_ref=src, dst_ref=dst, send_sem=send_sem, recv_sem=recv_sem, device_id=where, device_id_type=MESH
        )
        copy.start()
        sends.append(copy)

    for n, peer in enumerate(peers):
        send(delsrc.at[peer], dels.at[head], del_send.at[n], del_recv.at[head], {"head": peer})
    for n, peer in enumerate(peers):
        cols = pl.ds(pl.multiple_of(peer * 256, 256), 256)
        send(cotv.at[:, cols], cots.at[head], cot_send.at[n], cot_recv.at[head], {"head": peer})
        if n == 4:
            half = pl.ds(1024, 1024)
            send(k_hbm.at[0, half, :], kx.at[pl.ds(0, 1024), :], halo_send.at[0], halo_recv.at[0], {"ctx": nxt})
            send(v_hbm.at[0, half, :], vx.at[pl.ds(0, 1024), :], halo_send.at[1], halo_recv.at[1], {"ctx": nxt})
            first, past = pl.ds(0, 1024), pl.ds(2048, 1024)
            send(lse_hbm.at[:, first], lsev.at[:, past], halo_send.at[2], halo_recv.at[2], {"ctx": prv})
            send(doc_hbm.at[pl.ds(0, 8), :], docv.at[pl.ds(16, 8), :], halo_send.at[3], halo_recv.at[3], {"ctx": prv})
            send(q_hbm.at[:, first, :], qv.at[:, past, :], halo_send.at[4], halo_recv.at[4], {"ctx": prv})

    cots[head] = cotv[:, pl.ds(pl.multiple_of(head * 256, 256), 256)]
    dels[head] = delsrc[head]
    dka[...] = jnp.zeros_like(dka)
    dva[...] = jnp.zeros_like(dva)

    def waiting(dst, recv_sem, where):
        pltpu.make_async_remote_copy(
            src_ref=dst, dst_ref=dst, send_sem=cot_send.at[0], recv_sem=recv_sem, device_id=where, device_id_type=MESH
        ).wait_recv()

    base = ctx * 2048
    col = lax.broadcasted_iota(jnp.int32, (1, 128), 1)

    def queries_of(q0):
        return jnp.concatenate([qv[0, pl.ds(q0, 128), :], qv[1, pl.ds(q0, 128), :]], axis=0)

    def make_probs(pair, rows, far):
        for which in range(2):
            chunk = pair * 2 + which
            q0 = pl.multiple_of(chunk * 128, 128)
            query = queries_of(q0)
            at = pl.ds(q0, 128)
            lse = jnp.concatenate([lsev[0:1, at], lsev[1:2, at]], axis=1) * LOG2E
            low = jnp.maximum(docv[pl.ds(chunk, 1), :] - base + (W - q0), col + 1) + far
            low = jnp.concatenate([low, low], axis=1)
            high = jnp.concatenate([col, col], axis=1) + W
            span = min(1152, rows - 128 * which)
            for first, count in ((0, min(span, 1024)), (1024, span - 1024)):
                if count <= 0:
                    continue
                scores = mm(kx[pl.ds(q0 + first, count), :], query, NT)
                row = lax.broadcasted_iota(jnp.int32, (count, 256), 0) + first
                allowed = row >= low
                if first == 1024:
                    allowed = allowed & (row <= high)
                value = jnp.where(allowed, jnp.exp2(scores * (SCALE * LOG2E) - lse), 0.0)
                probs[pair, pl.ds(128 * which + first, count), pl.ds(256 * which, 256)] = value

    def use_pair(pair, rows, with_queries):
        q0 = pl.multiple_of(pair * 256, 256)
        query, cot, delta, grads = [], [], [], [[], []]
        for which in range(2):
            chunk = pair * 2 + which
            query.append(queries_of(q0 + 128 * which))
            block = cots[chunk]
            cot.append(jnp.concatenate([block[:, :128], block[:, 128:]], axis=0))
            both = dels[chunk]
            delta.append(jnp.concatenate([both[0:1], both[1:2]], axis=1))
        for first, count, whom in segments(rows):
            at = pl.ds(q0 + first, count)
            used = [w for w in range(2) if "AB"[w] in whom]
            low_probs, low_scores = [], []
            for w in used:
                prob = probs[pair, pl.ds(first, count), pl.ds(256 * w, 256)]
                dprobs = mm(vx[at, :], cot[w], NT)
                dscores = (prob * (dprobs - delta[w])).astype(BF)
                low_probs.append(prob.astype(BF))
                low_scores.append(dscores)
                if with_queries:
                    grads[w].append(mm(kt[:, at], dscores, NN))
            dva[at, :] += mm(side(low_probs, 1), side([cot[w] for w in used], 0), NN)
            dka[at, :] += mm(side(low_scores, 1), side([query[w] for w in used], 0), NN)
        if with_queries:
            for w in range(2):
                total = functools.reduce(jnp.add, grads[w]).T
                total = (total * SCALE).astype(BF)
                at = pl.ds(q0 + 128 * w, 128)
                dqo[0, at, :] = total[:128]
                dqo[1, at, :] = total[128:]

    for load in loads[2:]:
        load.wait()
    for b in range(8, 24):
        kt[:, b * 128 : (b + 1) * 128] = kx[pl.ds(b * 128, 128), :].T

    @pl.loop(4, 8)
    def _(pair):
        make_probs(pair, 1280, 0)

    to_next, to_prev = {"ctx": nxt}, {"ctx": prv}
    waiting(kx.at[pl.ds(0, 1024), :], halo_recv.at[0], to_next)
    for b in range(8):
        kt[:, b * 128 : (b + 1) * 128] = kx[pl.ds(b * 128, 128), :].T

    @pl.loop(0, 4)
    def _(pair):
        make_probs(pair, 1280, 0)

    waiting(lsev.at[:, pl.ds(2048, 1024)], halo_recv.at[2], to_prev)
    waiting(docv.at[pl.ds(16, 8), :], halo_recv.at[3], to_prev)
    waiting(qv.at[:, pl.ds(2048, 1024), :], halo_recv.at[4], to_prev)
    beyond = jnp.where(ctx == 15, 1 << 20, 0)
    for k in range(4):
        make_probs(8 + k, 1024 - 256 * k, beyond)
    waiting(vx.at[pl.ds(0, 1024), :], halo_recv.at[1], to_next)

    def source(step):
        far = (step + 1) // 2
        return lax.rem(z + jnp.where(step % 2 == 1, 8 - far, far), 8)

    def forward(pair, start):
        two = pl.ds(pair * 2, 2)
        past = pl.ds(16 + pair * 2, 2)
        for src, dst, ssem, rsem in (
            (dels.at[two], dels.at[past], fwd_del_send.at[pair], fwd_del_recv.at[pair]),
            (cots.at[two], cots.at[past], fwd_send.at[pair], fwd_recv.at[pair]),
        ):
            copy = pltpu.make_async_remote_copy(
                src_ref=src, dst_ref=dst, send_sem=ssem, recv_sem=rsem, device_id=to_prev, device_id_type=MESH
            )
            if start:
                copy.start()
            else:
                copy.wait_send()

    def store(pair):
        at = pl.ds(pl.multiple_of(pair * 256, 256), 256)
        return pltpu.make_async_copy(dqo.at[:, at, :], dq_hbm.at[:, at, :], store_sem.at[pair])

    @pl.loop(0, 9)
    def _(step):
        @pl.when(step < 8)
        def _():
            pair = source(step)
            for w in range(2):
                sender = pair * 2 + w

                @pl.when(sender != head)
                def _():
                    waiting(dels.at[sender], del_recv.at[sender], {"head": peers[0]})
                    waiting(cots.at[sender], cot_recv.at[sender], {"head": peers[0]})

            @pl.when(pair < 4)
            def _():
                forward(pair, True)

            use_pair(pair, 1280, True)
            store(pair).start()

        @pl.when(step > 0)
        def _():
            pair = source(step - 1)
            for k in range(4):

                @pl.when(pair == k)
                def _():
                    past = pl.ds(16 + k * 2, 2)
                    waiting(dels.at[past], fwd_del_recv.at[k], to_prev)
                    waiting(cots.at[past], fwd_recv.at[k], to_prev)
                    use_pair(8 + k, 1024 - 256 * k, False)

    dko[...] = (dka[pl.ds(1024, 2048), :] * SCALE).astype(BF)
    dvo[...] = dva[pl.ds(1024, 2048), :].astype(BF)
    stores = [
        pltpu.make_async_copy(dko, dk_hbm.at[0], store_sem.at[8]),
        pltpu.make_async_copy(dvo, dv_hbm.at[0], store_sem.at[9]),
    ]
    for copy in stores:
        copy.start()
    for copy in sends:
        copy.wait_send()
    for k in range(4):
        forward(k, False)
    for pair in range(8):
        store(pair).wait()
    for copy in stores:
        copy.wait()


def body(queries, key_states, value_states, attn_output, out_cotangent, logsumexp, doc_start):
    hbm = pl.BlockSpec(memory_space=pl.ANY)
    dma = pltpu.SemaphoreType.DMA
    return pl.pallas_call(
        attention_kernel,
        name="attention_backward",
        out_shape=(
            jax.ShapeDtypeStruct((2, 2048, 128), BF),
            jax.ShapeDtypeStruct((1, 2048, 128), BF),
            jax.ShapeDtypeStruct((1, 2048, 128), BF),
        ),
        in_specs=[hbm] * 7,
        out_specs=(hbm, hbm, hbm),
        scratch_shapes=[
            pltpu.VMEM((2, 3072, 128), BF),
            pltpu.VMEM((3072, 128), BF),
            pltpu.VMEM((3072, 128), BF),
            pltpu.VMEM((128, 3072), BF),
            pltpu.VMEM((128, 4096), BF),
            pltpu.VMEM((128, 4096), BF),
            pltpu.VMEM((2, 3072), F32),
            pltpu.VMEM((24, 128), jnp.int32),
            pltpu.VMEM((24, 128, 256), BF),
            pltpu.VMEM((24, 2, 128), F32),
            pltpu.VMEM((16, 2, 128), F32),
            pltpu.VMEM((12, 1280, 512), F32),
            pltpu.VMEM((3072, 128), F32),
            pltpu.VMEM((3072, 128), F32),
            pltpu.VMEM((2, 2048, 128), BF),
            pltpu.VMEM((2048, 128), BF),
            pltpu.VMEM((2048, 128), BF),
            dma((7,)), dma((5,)), dma((5,)), dma((15,)), dma((16,)), dma((15,)), dma((16,)),
            dma((4,)), dma((4,)), dma((4,)), dma((4,)), dma((10,)),
        ],
        compiler_params=pltpu.CompilerParams(collective_id=0, has_side_effects=True, vmem_limit_bytes=58 << 20),
    )(queries, key_states, value_states, attn_output, out_cotangent, logsumexp, doc_start.reshape(16, 128))


def solution(mesh):
    return jax.shard_map(
        body,
        mesh=mesh,
        in_specs=(
            P("head", "ctx", None),
            P("head", "ctx", None),
            P("head", "ctx", None),
            P(("ctx", "head"), None),
            P(("ctx", "head"), None),
            P("head", "ctx"),
            P("ctx"),
        ),
        out_specs=(P("head", "ctx", None), P("head", "ctx", None), P("head", "ctx", None)),
        check_vma=False,
    )
```

time: 146 us -> 51.8 us (0.35)
  Pallas kernels: 0 us -> 46.7 us
  waiting for transfers between devices: 44.1 us -> 0 us
  matrix products: 33.7 us -> 0 us
  starting transfers between devices: 31.9 us -> 0 us
  other arithmetic: 14.9 us -> 0 us
  local copies, waits for them, and re-layouts: 18.9 us -> 4.35 us
    pallas_call x0 -> x1, Pallas kernels: none -> 46.7 us  [body(): pl.pallas_call(attention_kernel, name='attention_backward', out_shape=(ja...]
    dot_general x20 -> x0, matrix products: 33.7 us -> none  [the longest x4 10.1 us: band_tile(): jnp.einsum('rkgd,kjd->kgrj', cotan_block, value_block, preferred_element_...]
    all_to_all x2 -> x0, waiting for transfers between devices: 30.8 us -> none  [the longest x1 23 us: body(): lax.all_to_all(seq_cotan, 'head', split_axis=1, concat_axis=0, tiled=True)]
    ppermute x4 -> x0, starting transfers between devices: 16.1 us -> none  [from_behind(): return lax.ppermute(block, axis, route)]
    all_to_all x2 -> x0, starting transfers between devices: 15.8 us -> none  [the longest x1 9.35 us: body(): lax.all_to_all(seq_cotan, 'head', split_axis=1, concat_axis=0, tiled=True)]
    ppermute x4 -> x0, waiting for transfers between devices: 13.3 us -> none  [from_behind(): return lax.ppermute(block, axis, route)]
    and x4 -> x0, other arithmetic: 5.14 us -> none  [block_step(): allowed = near & (key_local[None, :] >= start_rel[:, None])]
    concatenate x4 -> x0, other arithmetic: 3.65 us -> none  [the longest x1 1 us: body(): key_ext = jnp.concatenate([key_rim, key_states], axis=1)]
  transfers between devices with their start and end apart: 6 -> 0, of which waited for: 6 -> 0; matrix products, arithmetic and copies ran while one was open for 7% -> 0% of each run, Pallas kernels for 0% -> 0%
where the time goes in v1:
time: 51.8 us; the launch traced here: 51.7 us
  Pallas kernels  46.7 us (90%)
  local copies, waits for them, and re-layouts  4.35 us (8%)
  between operations  0.65 us (1%)
    pallas_call x1, Pallas kernels, body(): pl.pallas_call(attention_kernel, name='attention_backward', out_shape=(ja...  46.7 us
    unnamed x7, local copies, waits for them, and re-layouts  4.35 us

profile of v1, /device:TPU:25, one launch (start us, length us, event | category | flops | bytes accessed | tf_op | source)
XLA Modules:
  0.0 51.7 jit_solution(6000689389058918736)
XLA Ops:
  0.6 46.7 %attention_backward.1 = (bf16[2,2048,128]{2,1,0:T(8,128)(2,1)}, bf16[1,2048,128]{2,1,0:T(8,128)(2,1)}, bf16[1,2048,128]{2,1,0:T(8,128)(2,1)}) custom-call(bf16[2,2048,128]{2,1,0:T(8,128)(2,1)} %q_hbm.1, bf16[1,2048,128]{2,1,0:T(8,128)(2,1)} %k_hbm.1, bf16[1,2048,128]{2,1,0:T(8,128)(2,1)} %v_hbm.1, bf16[128,4096]{1,0:T(8,128)(2,1)} %out_hbm.1, ...), custom_call_target="tpu_custom_call" | custom-call | tf_op jit(solution)/shard_map/attention_backward/pallas_call | solution.py:275
  47.3 0.0 copy-start.1
  47.3 2.3 %copy.13 = bf16[2,2048,128]{2,1,0:T(8,128)(2,1)} copy(bf16[2,2048,128]{2,1,0:T(8,128)(2,1)} %get-tuple-element.6) | data formatting | bytes 2097152
  49.6 0.0 copy-done.1
  49.6 0.0 copy-start
  49.6 0.8 %copy.14 = bf16[1,2048,128]{2,1,0:T(8,128)(2,1)} copy(bf16[1,2048,128]{2,1,0:T(8,128)(2,1)S(1)} %copy-done.1) | data formatting | bytes 1048576
  50.4 0.4 copy-done
  50.9 0.8 %copy.15 = bf16[1,2048,128]{2,1,0:T(8,128)(2,1)} copy(bf16[1,2048,128]{2,1,0:T(8,128)(2,1)S(1)} %copy-done) | data formatting | bytes 1048576
Async XLA Ops:
  47.3 2.3 %copy-start.1 = (bf16[1,2048,128]{2,1,0:T(8,128)(2,1)S(1)}, bf16[1,2048,128]{2,1,0:T(8,128)(2,1)}, u32[]{:S(2)}) copy-start(bf16[1,2048,128]{2,1,0:T(8,128)(2,1)} %get-tuple-element.7) | copy-start | bytes 1572868
  49.6 1.2 %copy-start = (bf16[1,2048,128]{2,1,0:T(8,128)(2,1)S(1)}, bf16[1,2048,128]{2,1,0:T(8,128)(2,1)}, u32[]{:S(2)}) copy-start(bf16[1,2048,128]{2,1,0:T(8,128)(2,1)} %get-tuple-element.8) | copy-start | bytes 1572868

commit v2 on v1

--- a/solution.py
+++ b/solution.py
@@ -13,6 +13,7 @@
 LOG2E = 1.4426950408889634
 MESH = pl.DeviceIdType.MESH
 BF = jnp.bfloat16
+LAG = 4
 F32 = jnp.float32
 NT = (((1,), (1,)), ((), ()))
 NN = (((1,), (0,)), ((), ()))
@@ -35,10 +36,10 @@
 
 def attention_kernel(
     q_hbm, k_hbm, v_hbm, out_hbm, cot_hbm, lse_hbm, doc_hbm,
-    dq_hbm, dk_hbm, dv_hbm,
-    qv, kx, vx, kt, outv, cotv, lsev, docv, cots, dels, delsrc, probs, dka, dva, dqo, dko, dvo,
+    dqo, dko, dvo,
+    qv, kx, vx, kt, outv, cotv, lsev, docv, cots, dels, delsrc, probs, dka, dva,
     load_sem, halo_send, halo_recv, cot_send, cot_recv, del_send, del_recv,
-    fwd_send, fwd_recv, fwd_del_send, fwd_del_recv, store_sem,
+    fwd_send, fwd_recv, fwd_del_send, fwd_del_recv,
 ):
     ctx = lax.axis_index("ctx")
     head = lax.axis_index("head")
@@ -78,27 +79,51 @@
 
     pl.semaphore_wait(barrier, 17)
     sends = []
+    has_prev, has_next = ctx > 0, ctx < 15
+
+    def remote(src, dst, n, where):
+        return pltpu.make_async_remote_copy(
+            src_ref=src, dst_ref=dst, send_sem=halo_send.at[n], recv_sem=halo_recv.at[n], device_id=where, device_id_type=MESH
+        )
+
+    def halo_to_next():
+        last, before = pl.ds(1024, 1024), pl.ds(0, 1024)
+        return [
+            remote(k_hbm.at[0, last, :], kx.at[before, :], 0, {"ctx": nxt}),
+            remote(v_hbm.at[0, last, :], vx.at[before, :], 1, {"ctx": nxt}),
+        ]
+
+    def halo_to_prev():
+        first, past = pl.ds(0, 1024), pl.ds(2048, 1024)
+        return [
+            remote(lse_hbm.at[:, first], lsev.at[:, past], 2, {"ctx": prv}),
+            remote(doc_hbm.at[pl.ds(0, 8), :], docv.at[pl.ds(16, 8), :], 3, {"ctx": prv}),
+            remote(q_hbm.at[:, first, :], qv.at[:, past, :], 4, {"ctx": prv}),
+        ]
 
     def send(src, dst, send_sem, recv_sem, where):
         copy = pltpu.make_async_remote_copy(
             src_ref=src, dst_ref=dst, send_sem=send_sem, recv_sem=recv_sem, device_id=where, device_id_type=MESH
         )
         copy.start()
-        sends.append(copy)
+        return copy
 
     for n, peer in enumerate(peers):
-        send(delsrc.at[peer], dels.at[head], del_send.at[n], del_recv.at[head], {"head": peer})
+        sends.append(send(delsrc.at[peer], dels.at[head], del_send.at[n], del_recv.at[head], {"head": peer}))
     for n, peer in enumerate(peers):
         cols = pl.ds(pl.multiple_of(peer * 256, 256), 256)
-        send(cotv.at[:, cols], cots.at[head], cot_send.at[n], cot_recv.at[head], {"head": peer})
+        sends.append(send(cotv.at[:, cols], cots.at[head], cot_send.at[n], cot_recv.at[head], {"head": peer}))
         if n == 4:
-            half = pl.ds(1024, 1024)
-            send(k_hbm.at[0, half, :], kx.at[pl.ds(0, 1024), :], halo_send.at[0], halo_recv.at[0], {"ctx": nxt})
-            send(v_hbm.at[0, half, :], vx.at[pl.ds(0, 1024), :], halo_send.at[1], halo_recv.at[1], {"ctx": nxt})
-            first, past = pl.ds(0, 1024), pl.ds(2048, 1024)
-            send(lse_hbm.at[:, first], lsev.at[:, past], halo_send.at[2], halo_recv.at[2], {"ctx": prv})
-            send(doc_hbm.at[pl.ds(0, 8), :], docv.at[pl.ds(16, 8), :], halo_send.at[3], halo_recv.at[3], {"ctx": prv})
-            send(q_hbm.at[:, first, :], qv.at[:, past, :], halo_send.at[4], halo_recv.at[4], {"ctx": prv})
+
+            @pl.when(has_next)
+            def _():
+                for copy in halo_to_next():
+                    copy.start()
+
+            @pl.when(has_prev)
+            def _():
+                for copy in halo_to_prev():
+                    copy.start()
 
     cots[head] = cotv[:, pl.ds(pl.multiple_of(head * 256, 256), 256)]
     dels[head] = delsrc[head]
@@ -116,14 +141,14 @@
     def queries_of(q0):
         return jnp.concatenate([qv[0, pl.ds(q0, 128), :], qv[1, pl.ds(q0, 128), :]], axis=0)
 
-    def make_probs(pair, rows, far):
+    def make_probs(pair, rows):
         for which in range(2):
             chunk = pair * 2 + which
             q0 = pl.multiple_of(chunk * 128, 128)
             query = queries_of(q0)
             at = pl.ds(q0, 128)
             lse = jnp.concatenate([lsev[0:1, at], lsev[1:2, at]], axis=1) * LOG2E
-            low = jnp.maximum(docv[pl.ds(chunk, 1), :] - base + (W - q0), col + 1) + far
+            low = jnp.maximum(docv[pl.ds(chunk, 1), :] - base + (W - q0), col + 1)
             low = jnp.concatenate([low, low], axis=1)
             high = jnp.concatenate([col, col], axis=1) + W
             span = min(1152, rows - 128 * which)
@@ -177,24 +202,37 @@
 
     @pl.loop(4, 8)
     def _(pair):
-        make_probs(pair, 1280, 0)
+        make_probs(pair, 1280)
 
     to_next, to_prev = {"ctx": nxt}, {"ctx": prv}
-    waiting(kx.at[pl.ds(0, 1024), :], halo_recv.at[0], to_next)
+
+    @pl.when(has_prev)
+    def _():
+        waiting(kx.at[pl.ds(0, 1024), :], halo_recv.at[0], to_next)
+
+    @pl.when(jnp.logical_not(has_prev))
+    def _():
+        kx[pl.ds(0, 1024), :] = jnp.zeros((1024, 128), BF)
+        vx[pl.ds(0, 1024), :] = jnp.zeros((1024, 128), BF)
+
     for b in range(8):
         kt[:, b * 128 : (b + 1) * 128] = kx[pl.ds(b * 128, 128), :].T
 
     @pl.loop(0, 4)
     def _(pair):
-        make_probs(pair, 1280, 0)
-
-    waiting(lsev.at[:, pl.ds(2048, 1024)], halo_recv.at[2], to_prev)
-    waiting(docv.at[pl.ds(16, 8), :], halo_recv.at[3], to_prev)
-    waiting(qv.at[:, pl.ds(2048, 1024), :], halo_recv.at[4], to_prev)
-    beyond = jnp.where(ctx == 15, 1 << 20, 0)
-    for k in range(4):
-        make_probs(8 + k, 1024 - 256 * k, beyond)
-    waiting(vx.at[pl.ds(0, 1024), :], halo_recv.at[1], to_next)
+        make_probs(pair, 1280)
+
+    @pl.when(has_next)
+    def _():
+        waiting(lsev.at[:, pl.ds(2048, 1024)], halo_recv.at[2], to_prev)
+        waiting(docv.at[pl.ds(16, 8), :], halo_recv.at[3], to_prev)
+        waiting(qv.at[:, pl.ds(2048, 1024), :], halo_recv.at[4], to_prev)
+        for k in range(4):
+            make_probs(8 + k, 1024 - 256 * k)
+
+    @pl.when(has_prev)
+    def _():
+        waiting(vx.at[pl.ds(0, 1024), :], halo_recv.at[1], to_next)
 
     def source(step):
         far = (step + 1) // 2
@@ -215,11 +253,7 @@
             else:
                 copy.wait_send()
 
-    def store(pair):
-        at = pl.ds(pl.multiple_of(pair * 256, 256), 256)
-        return pltpu.make_async_copy(dqo.at[:, at, :], dq_hbm.at[:, at, :], store_sem.at[pair])
-
-    @pl.loop(0, 9)
+    @pl.loop(0, 8 + LAG)
     def _(step):
         @pl.when(step < 8)
         def _():
@@ -232,16 +266,15 @@
                     waiting(dels.at[sender], del_recv.at[sender], {"head": peers[0]})
                     waiting(cots.at[sender], cot_recv.at[sender], {"head": peers[0]})
 
-            @pl.when(pair < 4)
+            @pl.when(has_prev & (pair < 4))
             def _():
                 forward(pair, True)
 
             use_pair(pair, 1280, True)
-            store(pair).start()
-
-        @pl.when(step > 0)
+
+        @pl.when(has_next & (step >= LAG))
         def _():
-            pair = source(step - 1)
+            pair = source(step - LAG)
             for k in range(4):
 
                 @pl.when(pair == k)
@@ -253,35 +286,43 @@
 
     dko[...] = (dka[pl.ds(1024, 2048), :] * SCALE).astype(BF)
     dvo[...] = dva[pl.ds(1024, 2048), :].astype(BF)
-    stores = [
-        pltpu.make_async_copy(dko, dk_hbm.at[0], store_sem.at[8]),
-        pltpu.make_async_copy(dvo, dv_hbm.at[0], store_sem.at[9]),
-    ]
-    for copy in stores:
-        copy.start()
     for copy in sends:
         copy.wait_send()
-    for k in range(4):
-        forward(k, False)
-    for pair in range(8):
-        store(pair).wait()
-    for copy in stores:
+
+    @pl.when(has_next)
+    def _():
+        for copy in halo_to_next():
+            copy.wait_send()
+
+    @pl.when(has_prev)
+    def _():
+        for copy in halo_to_prev():
+            copy.wait_send()
+        for k in range(4):
+            forward(k, False)
+
+
+def write_kernel(dq, dk, dv, dq_hbm, dk_hbm, dv_hbm, sem):
+    copies = [
+        pltpu.make_async_copy(src, dst, sem.at[n])
+        for n, (src, dst) in enumerate(((dq, dq_hbm), (dk, dk_hbm.at[0]), (dv, dv_hbm.at[0])))
+    ]
+    for copy in copies:
+        copy.start()
+    for copy in copies:
         copy.wait()
 
 
 def body(queries, key_states, value_states, attn_output, out_cotangent, logsumexp, doc_start):
     hbm = pl.BlockSpec(memory_space=pl.ANY)
     dma = pltpu.SemaphoreType.DMA
-    return pl.pallas_call(
+    vmem = pl.BlockSpec(memory_space=pltpu.VMEM)
+    grads = pl.pallas_call(
         attention_kernel,
         name="attention_backward",
-        out_shape=(
-            jax.ShapeDtypeStruct((2, 2048, 128), BF),
-            jax.ShapeDtypeStruct((1, 2048, 128), BF),
-            jax.ShapeDtypeStruct((1, 2048, 128), BF),
-        ),
+        out_shape=(pltpu.VMEM((2, 2048, 128), BF), pltpu.VMEM((2048, 128), BF), pltpu.VMEM((2048, 128), BF)),
         in_specs=[hbm] * 7,
-        out_specs=(hbm, hbm, hbm),
+        out_specs=(vmem, vmem, vmem),
         scratch_shapes=[
             pltpu.VMEM((2, 3072, 128), BF),
             pltpu.VMEM((3072, 128), BF),
@@ -297,14 +338,23 @@
             pltpu.VMEM((12, 1280, 512), F32),
             pltpu.VMEM((3072, 128), F32),
             pltpu.VMEM((3072, 128), F32),
-            pltpu.VMEM((2, 2048, 128), BF),
-            pltpu.VMEM((2048, 128), BF),
-            pltpu.VMEM((2048, 128), BF),
             dma((7,)), dma((5,)), dma((5,)), dma((15,)), dma((16,)), dma((15,)), dma((16,)),
-            dma((4,)), dma((4,)), dma((4,)), dma((4,)), dma((10,)),
+            dma((4,)), dma((4,)), dma((4,)), dma((4,)),
         ],
-        compiler_params=pltpu.CompilerParams(collective_id=0, has_side_effects=True, vmem_limit_bytes=58 << 20),
+        compiler_params=pltpu.CompilerParams(collective_id=0, has_side_effects=True, vmem_limit_bytes=56 << 20),
     )(queries, key_states, value_states, attn_output, out_cotangent, logsumexp, doc_start.reshape(16, 128))
+    return pl.pallas_call(
+        write_kernel,
+        name="write_gradients",
+        out_shape=(
+            jax.ShapeDtypeStruct((2, 2048, 128), BF),
+            jax.ShapeDtypeStruct((1, 2048, 128), BF),
+            jax.ShapeDtypeStruct((1, 2048, 128), BF),
+        ),
+        in_specs=[vmem] * 3,
+        out_specs=(hbm, hbm, hbm),
+        scratch_shapes=[dma((3,))],
+    )(*[pltpu.with_memory_space_constraint(grad, pltpu.VMEM) for grad in grads])
 
 
 def solution(mesh):

time: 51.8 us -> 45.9 us (0.89)
  the two profiles are of different devices: /device:TPU:25 before, /device:TPU:57 now
where the time goes in v2:
time: 45.9 us; the launch traced here: 45.8 us
  Pallas kernels  45.2 us (98%)
  between operations  0.64 us (1%)
    pallas_call x1, Pallas kernels, body(): pl.pallas_call(attention_kernel, name='attention_backward', out_shape=(pl...  43.8 us
    pallas_call x1, Pallas kernels, body(): pl.pallas_call(write_kernel, name='write_gradients', out_shape=(jax.Shape...  1.34 us

profile of v2, /device:TPU:57, one launch (start us, length us, event | category | flops | bytes accessed | tf_op | source)
XLA Modules:
  0.0 45.8 jit_solution(8497587672715332573)
XLA Ops:
  0.6 43.8 %attention_backward.1 = (bf16[2,2048,128]{2,1,0:T(8,128)(2,1)S(1)}, bf16[2048,128]{1,0:T(8,128)(2,1)S(1)}, bf16[2048,128]{1,0:T(8,128)(2,1)S(1)}) custom-call(bf16[2,2048,128]{2,1,0:T(8,128)(2,1)} %q_hbm.1, bf16[1,2048,128]{2,1,0:T(8,128)(2,1)} %k_hbm.1, bf16[1,2048,128]{2,1,0:T(8,128)(2,1)} %v_hbm.1, bf16[128,4096]{1,0:T(8,128)(2,1)} %out_hbm.1, ...), custom_call_target="tpu_custom_call" | custom-call | tf_op jit(solution)/shard_map/attention_backward/pallas_call | solution.py:320
  44.5 1.3 %write_gradients.1 = (bf16[2,2048,128]{2,1,0:T(8,128)(2,1)}, bf16[1,2048,128]{2,1,0:T(8,128)(2,1)}, bf16[1,2048,128]{2,1,0:T(8,128)(2,1)}) custom-call(bf16[2,2048,128]{2,1,0:T(8,128)(2,1)S(1)} %get-tuple-element.6.dq, bf16[2048,128]{1,0:T(8,128)(2,1)S(1)} %get-tuple-element.7.dk, bf16[2048,128]{1,0:T(8,128)(2,1)S(1)} %get-tuple-element.8.dv), custom_call_target="tpu_custom_call" | custom-call | tf_op jit(solution)/shard_map/write_gradients/pallas_call | solution.py:346

commit v3 on v2

v3 whole, which is shorter than its diff:
```python
import jax
import jax.numpy as jnp
from jax import lax
from jax.experimental import pallas as pl
from jax.experimental.pallas import tpu as pltpu
from jax.sharding import PartitionSpec as P

W = 1024
QPRE = 168
SCALE = QPRE ** (-0.5)
LOG2E = 1.4426950408889634
MESH = pl.DeviceIdType.MESH
BF = jnp.bfloat16
LAG = 8
PRE = 2
F32 = jnp.float32
NT = (((1,), (1,)), ((), ()))
NN = (((1,), (0,)), ((), ()))
PEERS = ((0, 0), (1, 0), (7, 0), (2, 0), (6, 0), (3, 0), (5, 0), (4, 0), (0, 1), (1, 1), (7, 1), (2, 1), (6, 1), (3, 1), (5, 1), (4, 1))


def mm(a, b, dims):
    return lax.dot_general(a, b, dims, preferred_element_type=F32)


def attention_kernel(
    q_hbm, k_hbm, v_hbm, out_hbm, cot_hbm, lse_hbm, doc_hbm,
    dqo, dko, dvo,
    qv, kx, vx, kt, outv, cotv, lsev, docv, cots, dels, delsrc, probs, dka, dva,
    load_sem, halo_send, halo_recv, cot_send, cot_recv, del_send, del_recv,
    fwd_send, fwd_recv,
):
    ctx = lax.axis_index("ctx")
    head = lax.axis_index("head")
    z, x = head // 2, head % 2
    nxt, prv = lax.rem(ctx + 1, 16), lax.rem(ctx + 15, 16)
    peers = [lax.rem(z + dz, 8) * 2 + lax.rem(x + dx, 2) for dz, dx in PEERS[1:]]

    barrier = pltpu.get_barrier_semaphore()
    for peer in peers:
        pl.semaphore_signal(barrier, inc=1, device_id={"head": peer}, device_id_type=MESH)
    for peer in (nxt, prv):
        pl.semaphore_signal(barrier, inc=1, device_id={"ctx": peer}, device_id_type=MESH)

    loads = [
        pltpu.make_async_copy(cot_hbm, cotv, load_sem.at[0]),
        pltpu.make_async_copy(out_hbm, outv, load_sem.at[1]),
        pltpu.make_async_copy(q_hbm, qv.at[:, pl.ds(0, 2048), :], load_sem.at[2]),
        pltpu.make_async_copy(k_hbm.at[0], kx.at[pl.ds(1024, 2048), :], load_sem.at[3]),
        pltpu.make_async_copy(v_hbm.at[0], vx.at[pl.ds(1024, 2048), :], load_sem.at[4]),
        pltpu.make_async_copy(lse_hbm, lsev.at[:, pl.ds(0, 2048)], load_sem.at[5]),
        pltpu.make_async_copy(doc_hbm, docv.at[pl.ds(0, 16), :], load_sem.at[6]),
    ]
    for load in loads:
        load.start()

    pl.semaphore_wait(barrier, 17)
    sends = []
    has_prev, has_next = ctx > 0, ctx < 15

    def remote(src, dst, n, where):
        return pltpu.make_async_remote_copy(
            src_ref=src, dst_ref=dst, send_sem=halo_send.at[n], recv_sem=halo_recv.at[n], device_id=where, device_id_type=MESH
        )

    def halo_to_next():
        last, before = pl.ds(1024, 1024), pl.ds(0, 1024)
        return [
            remote(k_hbm.at[0, last, :], kx.at[before, :], 0, {"ctx": nxt}),
            remote(v_hbm.at[0, last, :], vx.at[before, :], 1, {"ctx": nxt}),
        ]

    def halo_to_prev():
        first, past = pl.ds(0, 1024), pl.ds(2048, 1024)
        return [
            remote(lse_hbm.at[:, first], lsev.at[:, past], 2, {"ctx": prv}),
            remote(doc_hbm.at[pl.ds(0, 8), :], docv.at[pl.ds(16, 8), :], 3, {"ctx": prv}),
            remote(q_hbm.at[:, first, :], qv.at[:, past, :], 4, {"ctx": prv}),
        ]

    def send_past():
        @pl.when(has_prev)
        def _():
            for copy in halo_to_prev():
                copy.start()

    def send(src, dst, send_sem, recv_sem, where):
        copy = pltpu.make_async_remote_copy(
            src_ref=src, dst_ref=dst, send_sem=send_sem, recv_sem=recv_sem, device_id=where, device_id_type=MESH
        )
        copy.start()
        return copy

    def pick(step, values):
        picked = jnp.int32(0)
        for n, value in enumerate(values):
            picked = jnp.where(step == n, value, picked)
        return picked

    def block_copy(n):
        dz, dx = PEERS[n]
        peer = lax.rem(z + dz, 8) * 2 + lax.rem(x + dx, 2)
        return pltpu.make_async_remote_copy(
            src_ref=cot_hbm.at[:, pl.ds(pl.multiple_of(peer * 256, 256), 256)],
            dst_ref=cots.at[head],
            send_sem=cot_send.at[n - 1],
            recv_sem=cot_recv.at[head],
            device_id={"head": peer},
            device_id_type=MESH,
        )

    @pl.when(has_next)
    def _():
        for copy in halo_to_next():
            copy.start()

    for n in range(1, PRE + 1):
        block_copy(n).start()

    loads[0].wait()
    loads[1].wait()
    lane = lax.broadcasted_iota(jnp.int32, (128, 128), 1)
    rows_delta = jnp.zeros((128, 128), F32)
    for h in range(32):
        cols = slice(h * 128, (h + 1) * 128)
        product = cotv[:, cols].astype(F32) * outv[:, cols].astype(F32)
        rows_delta = jnp.where(lane == h, jnp.sum(product, axis=1, keepdims=True), rows_delta)
    rows_delta = rows_delta.T
    for j in range(16):
        delsrc[j] = rows_delta[2 * j : 2 * j + 2]

    for n, peer in enumerate(peers):
        sends.append(send(delsrc.at[peer], dels.at[head], del_send.at[n], del_recv.at[head], {"head": peer}))
    for n in range(PRE + 1, 16):
        block_copy(n).start()
    send_past()

    cots[head] = cotv[:, pl.ds(pl.multiple_of(head * 256, 256), 256)]
    dels[head] = delsrc[head]
    kx[pl.ds(3072, 128), :] = jnp.zeros((128, 128), BF)
    vx[pl.ds(3072, 128), :] = jnp.zeros((128, 128), BF)
    dka[...] = jnp.zeros_like(dka)
    dva[...] = jnp.zeros_like(dva)

    def waiting(dst, recv_sem, where):
        pltpu.make_async_remote_copy(
            src_ref=dst, dst_ref=dst, send_sem=cot_send.at[0], recv_sem=recv_sem, device_id=where, device_id_type=MESH
        ).wait_recv()

    base = ctx * 2048
    col = lax.broadcasted_iota(jnp.int32, (1, 128), 1)

    def queries_of(q0):
        return jnp.concatenate([qv[0, pl.ds(q0, 128), :], qv[1, pl.ds(q0, 128), :]], axis=0)

    def make_probs(chunk, span, keep):
        q0 = pl.multiple_of(chunk * 128, 128)
        query = queries_of(q0)
        at = pl.ds(q0, 128)
        lse = jnp.concatenate([lsev[0:1, at], lsev[1:2, at]], axis=1) * LOG2E
        low = jnp.maximum(docv[pl.ds(chunk, 1), :] - base + (W - q0), col + 1)
        low = jnp.concatenate([low, low], axis=1)
        high = jnp.concatenate([col, col], axis=1) + W
        for first, count in ((0, min(span, 1024)), (1024, span - 1024)):
            if count <= 0:
                continue
            scores = mm(kx[pl.ds(q0 + first, count), :], query, NT)
            row = lax.broadcasted_iota(jnp.int32, (count, 256), 0) + first
            allowed = row >= low
            if first == 1024:
                allowed = allowed & (row <= high)
            keep(first, count, jnp.where(allowed, jnp.exp2(scores * (SCALE * LOG2E) - lse), 0.0))

    def chunk_probs(chunk):
        def keep(first, count, value):
            probs[chunk, pl.ds(first, count), :] = value

        make_probs(chunk, 1152, keep)

    def cotangents_of(chunk):
        block = cots[chunk]
        return jnp.concatenate([block[:, :128], block[:, 128:]], axis=0)

    def delta_of(chunk):
        both = dels[chunk]
        return jnp.concatenate([both[0:1], both[1:2]], axis=1)

    def use_chunk(chunk):
        q0 = pl.multiple_of(chunk * 128, 128)
        query, cot, delta = queries_of(q0), cotangents_of(chunk), delta_of(chunk)
        at = pl.ds(q0, 1152)
        prob = probs[chunk]
        dscores = (prob * (mm(vx[at, :], cot, NT) - delta)).astype(BF)
        dva[at, :] += mm(prob.astype(BF), cot, NN)
        dka[at, :] += mm(dscores, query, NN)
        grad = (mm(kt[:, at], dscores, NN).T * SCALE).astype(BF)
        dqo[0, pl.ds(q0, 128), :] = grad[:128]
        dqo[1, pl.ds(q0, 128), :] = grad[128:]

    def use_past_chunk(chunk, rows):
        q0 = pl.multiple_of(2048 + chunk * 128, 128)
        query, cot, delta = queries_of(q0), cotangents_of(16 + chunk), delta_of(16 + chunk)
        at = pl.ds(q0, rows)

        def keep(first, count, prob):
            dscores = (prob * (mm(vx[at, :], cot, NT) - delta)).astype(BF)
            dva[at, :] += mm(prob.astype(BF), cot, NN)
            dka[at, :] += mm(dscores, query, NN)

        make_probs(16 + chunk, rows, keep)

    for load in loads[2:]:
        load.wait()
    for b in range(8, 24):
        kt[:, b * 128 : (b + 1) * 128] = kx[pl.ds(b * 128, 128), :].T

    @pl.loop(8, 16, unroll=2)
    def _(chunk):
        chunk_probs(chunk)

    to_next, to_prev = {"ctx": nxt}, {"ctx": prv}

    @pl.when(has_prev)
    def _():
        waiting(kx.at[pl.ds(0, 1024), :], halo_recv.at[0], to_next)

    @pl.when(jnp.logical_not(has_prev))
    def _():
        kx[pl.ds(0, 1024), :] = jnp.zeros((1024, 128), BF)
        vx[pl.ds(0, 1024), :] = jnp.zeros((1024, 128), BF)

    for b in range(8):
        kt[:, b * 128 : (b + 1) * 128] = kx[pl.ds(b * 128, 128), :].T

    @pl.loop(0, 8, unroll=2)
    def _(chunk):
        chunk_probs(chunk)

    @pl.when(has_prev)
    def _():
        waiting(vx.at[pl.ds(0, 1024), :], halo_recv.at[1], to_next)

    def source(step):
        back, across = pick(step, [8 - p[0] for p in PEERS]), pick(step, [p[1] for p in PEERS])
        return lax.rem(z + back, 8) * 2 + lax.rem(x + across, 2)

    def forward(chunk):
        return [
            pltpu.make_async_remote_copy(
                src_ref=ref.at[chunk],
                dst_ref=ref.at[16 + chunk],
                send_sem=fwd_send.at[n, chunk],
                recv_sem=fwd_recv.at[n, chunk],
                device_id=to_prev,
                device_id_type=MESH,
            )
            for n, ref in enumerate((dels, cots))
        ]

    @pl.loop(0, 16 + LAG)
    def _(step):
        @pl.when(step < 16)
        def _():
            chunk = source(step)

            @pl.when(chunk != head)
            def _():
                waiting(dels.at[chunk], del_recv.at[chunk], {"head": peers[0]})
                waiting(cots.at[chunk], cot_recv.at[chunk], {"head": peers[0]})

            @pl.when(has_prev & (chunk < 8))
            def _():
                for copy in forward(chunk):
                    copy.start()

            use_chunk(chunk)

        @pl.when(has_next & (step == LAG))
        def _():
            waiting(lsev.at[:, pl.ds(2048, 1024)], halo_recv.at[2], to_prev)
            waiting(docv.at[pl.ds(16, 8), :], halo_recv.at[3], to_prev)
            waiting(qv.at[:, pl.ds(2048, 1024), :], halo_recv.at[4], to_prev)

        @pl.when(has_next & (step >= LAG))
        def _():
            chunk = source(step - LAG)

            @pl.when(chunk < 8)
            def _():
                waiting(dels.at[16 + chunk], fwd_recv.at[0, chunk], to_prev)
                waiting(cots.at[16 + chunk], fwd_recv.at[1, chunk], to_prev)

            for k in range(4):

                @pl.when(chunk // 2 == k)
                def _():
                    use_past_chunk(chunk, 1024 - 256 * k)

    dko[...] = (dka[pl.ds(1024, 2048), :] * SCALE).astype(BF)
    dvo[...] = dva[pl.ds(1024, 2048), :].astype(BF)
    for copy in sends:
        copy.wait_send()
    for n in range(1, 16):
        block_copy(n).wait_send()

    @pl.when(has_next)
    def _():
        for copy in halo_to_next():
            copy.wait_send()

    @pl.when(has_prev)
    def _():
        for copy in halo_to_prev():
            copy.wait_send()
        for chunk in range(8):
            for copy in forward(chunk):
                copy.wait_send()


def write_kernel(dq, dk, dv, dq_hbm, dk_hbm, dv_hbm, sem):
    copies = [
        pltpu.make_async_copy(src, dst, sem.at[n])
        for n, (src, dst) in enumerate(((dq, dq_hbm), (dk, dk_hbm.at[0]), (dv, dv_hbm.at[0])))
    ]
    for copy in copies:
        copy.start()
    for copy in copies:
        copy.wait()


def body(queries, key_states, value_states, attn_output, out_cotangent, logsumexp, doc_start):
    hbm = pl.BlockSpec(memory_space=pl.ANY)
    dma = pltpu.SemaphoreType.DMA
    vmem = pl.BlockSpec(memory_space=pltpu.VMEM)
    grads = pl.pallas_call(
        attention_kernel,
        name="attention_backward",
        out_shape=(pltpu.VMEM((2, 2048, 128), BF), pltpu.VMEM((2048, 128), BF), pltpu.VMEM((2048, 128), BF)),
        in_specs=[hbm] * 7,
        out_specs=(vmem, vmem, vmem),
        scratch_shapes=[
            pltpu.VMEM((2, 3072, 128), BF),
            pltpu.VMEM((3200, 128), BF),
            pltpu.VMEM((3200, 128), BF),
            pltpu.VMEM((128, 3072), BF),
            pltpu.VMEM((128, 4096), BF),
            pltpu.VMEM((128, 4096), BF),
            pltpu.VMEM((2, 3072), F32),
            pltpu.VMEM((24, 128), jnp.int32),
            pltpu.VMEM((24, 128, 256), BF),
            pltpu.VMEM((24, 2, 128), F32),
            pltpu.VMEM((16, 2, 128), F32),
            pltpu.VMEM((16, 1152, 256), F32),
            pltpu.VMEM((3200, 128), F32),
            pltpu.VMEM((3200, 128), F32),
            dma((7,)), dma((5,)), dma((5,)), dma((15,)), dma((16,)), dma((15,)), dma((16,)),
            dma((2, 8)), dma((2, 8)),
        ],
        compiler_params=pltpu.CompilerParams(collective_id=0, has_side_effects=True, vmem_limit_bytes=56 << 20),
    )(queries, key_states, value_states, attn_output, out_cotangent, logsumexp, doc_start.reshape(16, 128))
    return pl.pallas_call(
        write_kernel,
        name="write_gradients",
        out_shape=(
            jax.ShapeDtypeStruct((2, 2048, 128), BF),
            jax.ShapeDtypeStruct((1, 2048, 128), BF),
            jax.ShapeDtypeStruct((1, 2048, 128), BF),
        ),
        in_specs=[vmem] * 3,
        out_specs=(hbm, hbm, hbm),
        scratch_shapes=[dma((3,))],
    )(*[pltpu.with_memory_space_constraint(grad, pltpu.VMEM) for grad in grads])


def solution(mesh):
    return jax.shard_map(
        body,
        mesh=mesh,
        in_specs=(
            P("head", "ctx", None),
            P("head", "ctx", None),
            P("head", "ctx", None),
            P(("ctx", "head"), None),
            P(("ctx", "head"), None),
            P("head", "ctx"),
            P("ctx"),
        ),
        out_specs=(P("head", "ctx", None), P("head", "ctx", None), P("head", "ctx", None)),
        check_vma=False,
    )
```

time: 45.9 us -> 42.3 us (0.922)
  the two profiles are of different devices: /device:TPU:57 before, /device:TPU:25 now
where the time goes in v3:
time: 42.3 us; the launch traced here: 42.2 us
  Pallas kernels  41.5 us (98%)
  between operations  0.64 us (2%)
    pallas_call x1, Pallas kernels, body(): pl.pallas_call(attention_kernel, name='attention_backward', out_shape=(pl...  40.2 us
    pallas_call x1, Pallas kernels, body(): pl.pallas_call(write_kernel, name='write_gradients', out_shape=(jax.Shape...  1.34 us

profile of v3, /device:TPU:25, one launch (start us, length us, event | category | flops | bytes accessed | tf_op | source)
XLA Modules:
  0.0 42.2 jit_solution(14898585858983217102)
XLA Ops:
  0.6 40.2 %attention_backward.1 = (bf16[2,2048,128]{2,1,0:T(8,128)(2,1)S(1)}, bf16[2048,128]{1,0:T(8,128)(2,1)S(1)}, bf16[2048,128]{1,0:T(8,128)(2,1)S(1)}) custom-call(bf16[2,2048,128]{2,1,0:T(8,128)(2,1)} %q_hbm.1, bf16[1,2048,128]{2,1,0:T(8,128)(2,1)} %k_hbm.1, bf16[1,2048,128]{2,1,0:T(8,128)(2,1)} %v_hbm.1, bf16[128,4096]{1,0:T(8,128)(2,1)} %out_hbm.1, ...), custom_call_target="tpu_custom_call" | custom-call | tf_op jit(solution)/shard_map/attention_backward/pallas_call | solution.py:335
  40.8 1.3 %write_gradients.1 = (bf16[2,2048,128]{2,1,0:T(8,128)(2,1)}, bf16[1,2048,128]{2,1,0:T(8,128)(2,1)}, bf16[1,2048,128]{2,1,0:T(8,128)(2,1)}) custom-call(bf16[2,2048,128]{2,1,0:T(8,128)(2,1)S(1)} %get-tuple-element.6.dq, bf16[2048,128]{1,0:T(8,128)(2,1)S(1)} %get-tuple-element.7.dk, bf16[2048,128]{1,0:T(8,128)(2,1)S(1)} %get-tuple-element.8.dv), custom_call_target="tpu_custom_call" | custom-call | tf_op jit(solution)/shard_map/write_gradients/pallas_call | solution.py:361

commit v4 on v3

--- a/solution.py
+++ b/solution.py
@@ -12,6 +12,7 @@
 MESH = pl.DeviceIdType.MESH
 BF = jnp.bfloat16
 LAG = 8
+PAST_AT = 3
 PRE = 2
 F32 = jnp.float32
 NT = (((1,), (1,)), ((), ()))
@@ -26,7 +27,7 @@
 def attention_kernel(
     q_hbm, k_hbm, v_hbm, out_hbm, cot_hbm, lse_hbm, doc_hbm,
     dqo, dko, dvo,
-    qv, kx, vx, kt, outv, cotv, lsev, docv, cots, dels, delsrc, probs, dka, dva,
+    qv, kx, vx, kt, outv, cotv, lsev, docv, cots, dels, delsrc, probs, past_probs, dka, dva,
     load_sem, halo_send, halo_recv, cot_send, cot_recv, del_send, del_recv,
     fwd_send, fwd_recv,
 ):
@@ -202,12 +203,16 @@
         query, cot, delta = queries_of(q0), cotangents_of(16 + chunk), delta_of(16 + chunk)
         at = pl.ds(q0, rows)
 
-        def keep(first, count, prob):
-            dscores = (prob * (mm(vx[at, :], cot, NT) - delta)).astype(BF)
-            dva[at, :] += mm(prob.astype(BF), cot, NN)
-            dka[at, :] += mm(dscores, query, NN)
-
-        make_probs(16 + chunk, rows, keep)
+        prob = past_probs[chunk, pl.ds(0, rows), :]
+        dscores = (prob * (mm(vx[at, :], cot, NT) - delta)).astype(BF)
+        dva[at, :] += mm(prob.astype(BF), cot, NN)
+        dka[at, :] += mm(dscores, query, NN)
+
+    def past_chunk_probs(chunk):
+        def keep(first, count, value):
+            past_probs[chunk, pl.ds(first, count), :] = value
+
+        make_probs(16 + chunk, 1024 - 256 * (chunk // 2), keep)
 
     for load in loads[2:]:
         load.wait()
@@ -275,11 +280,13 @@
 
             use_chunk(chunk)
 
-        @pl.when(has_next & (step == LAG))
+        @pl.when(has_next & (step == PAST_AT))
         def _():
             waiting(lsev.at[:, pl.ds(2048, 1024)], halo_recv.at[2], to_prev)
             waiting(docv.at[pl.ds(16, 8), :], halo_recv.at[3], to_prev)
             waiting(qv.at[:, pl.ds(2048, 1024), :], halo_recv.at[4], to_prev)
+            for chunk in range(8):
+                past_chunk_probs(chunk)
 
         @pl.when(has_next & (step >= LAG))
         def _():
@@ -351,6 +358,7 @@
             pltpu.VMEM((24, 2, 128), F32),
             pltpu.VMEM((16, 2, 128), F32),
             pltpu.VMEM((16, 1152, 256), F32),
+            pltpu.VMEM((8, 1024, 256), F32),
             pltpu.VMEM((3200, 128), F32),
             pltpu.VMEM((3200, 128), F32),
             dma((7,)), dma((5,)), dma((5,)), dma((15,)), dma((16,)), dma((15,)), dma((16,)),

time: 42.3 us -> 42.2 us (level)
  no operation moved by 1% of the time
where the time goes in v4:
time: 42.2 us; the launch traced here: 42.1 us
  Pallas kernels  41.5 us (98%)
  between operations  0.64 us (2%)
    pallas_call x1, Pallas kernels, body(): pl.pallas_call(attention_kernel, name='attention_backward', out_shape=(pl...  40.2 us
    pallas_call x1, Pallas kernels, body(): pl.pallas_call(write_kernel, name='write_gradients', out_shape=(jax.Shape...  1.34 us

profile of v4, /device:TPU:25, one launch (start us, length us, event | category | flops | bytes accessed | tf_op | source)
XLA Modules:
  0.0 42.1 jit_solution(5547979771673697356)
XLA Ops:
  0.6 40.2 %attention_backward.1 = (bf16[2,2048,128]{2,1,0:T(8,128)(2,1)S(1)}, bf16[2048,128]{1,0:T(8,128)(2,1)S(1)}, bf16[2048,128]{1,0:T(8,128)(2,1)S(1)}) custom-call(bf16[2,2048,128]{2,1,0:T(8,128)(2,1)} %q_hbm.1, bf16[1,2048,128]{2,1,0:T(8,128)(2,1)} %k_hbm.1, bf16[1,2048,128]{2,1,0:T(8,128)(2,1)} %v_hbm.1, bf16[128,4096]{1,0:T(8,128)(2,1)} %out_hbm.1, ...), custom_call_target="tpu_custom_call" | custom-call | tf_op jit(solution)/shard_map/attention_backward/pallas_call | solution.py:342
  40.8 1.3 %write_gradients.1 = (bf16[2,2048,128]{2,1,0:T(8,128)(2,1)}, bf16[1,2048,128]{2,1,0:T(8,128)(2,1)}, bf16[1,2048,128]{2,1,0:T(8,128)(2,1)}) custom-call(bf16[2,2048,128]{2,1,0:T(8,128)(2,1)S(1)} %get-tuple-element.6.dq, bf16[2048,128]{1,0:T(8,128)(2,1)S(1)} %get-tuple-element.7.dk, bf16[2048,128]{1,0:T(8,128)(2,1)S(1)} %get-tuple-element.8.dv), custom_call_target="tpu_custom_call" | custom-call | tf_op jit(solution)/shard_map/write_gradients/pallas_call | solution.py:369
